TPU v7x, 32 devices: a whole 2x2x4 slice. The times are simulated.
32 devices in a mesh: rows: 8 (over z, x), tm: 4 (over y, core).
Axes of the slice: x: 2, y: 2, z: 4, core: 2. Of those that a mesh axis runs over, the one named last changes fastest.
Arguments:
- snapshots: bfloat16 [262144, 512], P('rows', 'tm'), may hold values from -6 to 6
- modes: bfloat16 [262144, 256], P('rows'), may hold values from -0.01171875 to 0.01171875
- eig_vectors: float32 [3, 256], replicated, may hold values from -0.375 to 0.375
- eig_values: float32 [3], replicated, may hold values from -1 to 1
Outputs:
- operator: float32 [256, 256], replicated
- eig_residual: float32 [3, 256], replicated
- residual_norm: float32 [3], replicated
All inputs are finite; a program needn't handle non-finite values.
Results may differ from a plain program's by a relative error of at most 0.0003.
Values may be sent and summed in bfloat16 or wider, within the bound.
A program may use at most 128 MiB of HBM per device.

v0:
```python
import jax
import jax.numpy as jnp
from jax import lax
from jax.sharding import PartitionSpec as P


def pair_terms(coords, after, keep):
    lead = coords * keep
    trail = jnp.concatenate([coords[:, 1:], after], axis=1)
    cross_part = jnp.dot(
        trail, lead.T, precision=lax.Precision.HIGHEST, preferred_element_type=jnp.float32
    )
    gram_part = jnp.dot(
        lead, lead.T, precision=lax.Precision.HIGHEST, preferred_element_type=jnp.float32
    )
    return (cross_part, gram_part)


def body(snapshots, modes, eig_vectors, eig_values):
    block_cols = snapshots.shape[1]
    width = modes.shape[1]
    time_count = lax.axis_size("tm")
    total_cols = block_cols * time_count
    partial_value = jnp.einsum("mr,mt->rt", modes, snapshots, preferred_element_type=jnp.float32)
    coords = lax.psum(partial_value, "rows")
    series = lax.all_gather(coords, "tm", axis=1, tiled=True)
    every = lax.broadcasted_iota(jnp.int32, (1, total_cols), 1)
    whole_keep = (every < total_cols - 1).astype(jnp.float32)
    zero_col = jnp.zeros((width, 1), jnp.float32)
    cross, gram = pair_terms(series, zero_col, whole_keep)
    scale = jnp.float32(total_cols - 1)
    cross = cross / scale
    gram = gram / scale + jnp.eye(width, dtype=jnp.float32)
    factor = jnp.linalg.cholesky(gram)
    operator = jax.scipy.linalg.cho_solve((factor, True), cross.T).T
    eig_residual = (
        jnp.dot(
            eig_vectors,
            operator.T,
            precision=lax.Precision.HIGHEST,
            preferred_element_type=jnp.float32,
        )
        - eig_values[:, None] * eig_vectors
    )
    residual_norm = jnp.sqrt(jnp.sum(eig_residual * eig_residual, axis=1) + 1e-06)
    return (operator, eig_residual, residual_norm)


def solution(mesh):
    return jax.shard_map(
        body,
        mesh=mesh,
        in_specs=(P("rows", "tm"), P("rows", None), P(), P()),
        out_specs=(P(), P(), P()),
        check_vma=False,
    )
```

profile of v0, /device:TPU:0, one launch (start us, length us, event | category | flops | bytes accessed | tf_op | source)
XLA Modules:
  0.0 174.0 jit_solution(5392952128399339872)
XLA Ops:
  7.2 0.0 copy-start
  7.2 0.0 copy-start.1
  7.2 0.0 all-reduce.4.cloned.1.call-start
  7.2 13.4 %fusion.23 = f32[256,128]{1,0:T(8,128)} fusion(bf16[32768,256]{1,0:T(8,128)(2,1)} %param.5, bf16[32768,128]{1,0:T(8,128)(2,1)} %param.4), kind=kOutput, calls=%fused_computation.53 | convolution fusion | flops 2147483648 | bytes 25296896 | tf_op jit(solution)/shard_map/mr,mt->rt/dot_general | solution.py:24
  20.6 0.0 all-reduce.4.cloned.1.call-update
  20.7 73.3 %all-reduce.4.cloned.1.call-done = f32[256,128]{1,0:T(8,128)} async-done(((f32[256,128]{1,0:T(8,128)}), f32[256,128]{1,0:T(8,128)}) %all-reduce.4.cloned.1.call-update) | async-done | bytes 131088 | tf_op jit(solution)/shard_map/psum | solution.py:25
  94.0 7.5 %all_gather.3 = f32[256,512]{1,0:T(8,128)S(1)} all-gather(f32[256,128]{1,0:T(8,128)} %all-reduce.4.cloned.1.call-done), channel_id=1, replica_groups=mesh['rows'=8,'tm'=4] {'tm'}, dimensions={1}, use_global_device_ids=true | all-gather | bytes 655360 | tf_op jit(solution)/shard_map/all_gather | solution.py:26
  101.5 0.2 slice.77
  101.7 0.6 convert_add_fusion
  102.4 0.6 convolution_multiply_fusion
  103.0 0.1 copy.8
  103.2 11.7 %cholesky.50 = f32[128,128]{1,0:T(8,128)S(1)} custom-call(f32[128,128]{1,0:T(8,128)S(1)} %cholesky.118), custom_call_target="Cholesky" | custom-call | tf_op jit(solution)/shard_map/jit(cholesky)/cholesky | solution.py:34
  115.0 9.8 %custom-call.18 = f32[1,128,128]{1,2,0:T(8,128)S(1)} custom-call(f32[1,128,128]{2,1,0:T(8,128)S(1)} %get-tuple-element.27), custom_call_target="InvertDiagBlocksLowerTriangular" | custom-call | tf_op jit(solution)/shard_map/jit(cholesky)/cholesky | solution.py:34
  124.8 0.2 constant_dynamic-update-slice_fusion.1
  125.0 0.3 convolution_subtract_fusion.2
  125.3 11.7 %cholesky.105 = f32[128,128]{1,0:T(8,128)S(1)} custom-call(f32[128,128]{1,0:T(8,128)S(1)} %convolution_subtract_fusion.2), custom_call_target="Cholesky" | custom-call | tf_op jit(solution)/shard_map/jit(cholesky)/cholesky | solution.py:34
  137.0 0.6 compare_reduce_fusion
  139.0 0.1 triangular_solve.72
  139.1 4.2 %while.1 = (s32[]{:T(128)}, f32[256,256]{1,0:T(8,128)S(1)}, s32[2,2]{1,0:T(2,128)S(1)}, f32[2,128,128]{2,1,0:T(8,128)S(1)}, s32[]{:T(128)}) while((s32[]{:T(128)}, f32[256,256]{1,0:T(8,128)S(1)}, s32[2,2]{1,0:T(2,128)S(1)}, f32[2,128,128]{2,1,0:T(8,128)S(1)}, s32[]{:T(128)}) %tuple.30), condition=%wide.while_cond, body=%wide.while_body.sunk | while | flops 2 | bytes 131189 | solution.py:35
  139.3 0.6 fusion.35
  139.9 1.4 bitcast_dynamic-update-slice_fusion.2
  141.3 0.6 fusion.35
  141.9 1.4 bitcast_dynamic-update-slice_fusion.2
  143.3 19.7 %custom-call.19 = f32[2,128,128]{1,2,0:T(8,128)S(1)} custom-call(f32[2,128,128]{2,1,0:T(8,128)S(1)} %get-tuple-element.10), custom_call_target="InvertDiagBlocksLowerTriangular" | custom-call | tf_op jit(solution)/shard_map/jit(_cho_solve)/triangular_solve | solution.py:35
  162.9 0.3 fusion.9
  163.3 0.4 convolution_subtract_fusion.1
  163.7 0.3 fusion.16
  164.0 0.3 fusion.15
  164.2 0.3 convolution_subtract_fusion
  164.6 0.3 fusion.14
  164.9 0.8 copy.10
  165.7 0.0 copy-done
  165.7 0.0 copy-done.1
  165.7 1.0 multiply_reduce_fusion
  166.7 0.5 add_sqrt_fusion
  (12 shorter events, 0.2 us)
Async XLA Ops:
  7.2 158.5 %copy-start = (f32[3,256]{1,0:T(4,128)S(1)}, f32[3,256]{1,0:T(4,128)}, u32[]{:S(2)}) copy-start(f32[3,256]{1,0:T(4,128)} %param.6) | copy-start | bytes 9220
  7.2 158.5 %copy-start.1 = (f32[3]{0:T(128)S(1)}, f32[3]{0:T(128)}, u32[]{:S(2)}) copy-start(f32[3]{0:T(128)} %param.7) | copy-start | bytes 40
  7.2 86.8 %all-reduce.4.cloned.1.call-start = ((), (), s32[]{:S(2)}) async-start(), calls=%async_computation | async-start | bytes 262144 | tf_op jit(solution)/shard_map/psum | solution.py:25
Sparse Core Ops, SparseCore 0:
  20.8 73.1 all-reduce.3
where the time goes:
time: 174 us
  waiting for transfers between devices  73.3 us (42%)
  other arithmetic  54.2 us (31%)
  matrix products  17.9 us (10%)
  between operations  15.5 us (9%)
  blocking collectives  7.53 us (4%)
  local copies, waits for them, and re-layouts  5.22 us (3%)
    psum x1, waiting for transfers between devices, body(): coords = lax.psum(partial_value, 'rows')  73.3 us
    another operation x6, other arithmetic, body(): factor = jnp.linalg.cholesky(gram)  33.9 us
    another operation x3, other arithmetic, body(): operator = jax.scipy.linalg.cho_solve((factor, True), cross.T).T  19.7 us
    dot_general x1, matrix products, body(): jnp.einsum('mr,mt->rt', modes, snapshots, preferred_element_type=jnp.floa...  13.4 us
    all_gather x1, blocking collectives, body(): series = lax.all_gather(coords, 'tm', axis=1, tiled=True)  7.53 us
    another operation x6, local copies, waits for them, and re-layouts  3.95 us
  transfers between devices with their start and end apart: 1, of which 1 were waited for; matrix products, arithmetic and copies ran while one was open for 0% of the time, Pallas kernels for 0%

commit v1 on v0

v1 whole, which is shorter than its diff:
```python
import functools

import jax
import jax.numpy as jnp
from jax import lax
from jax.experimental import pallas as pl
from jax.experimental.pallas import tpu as pltpu
from jax.sharding import PartitionSpec as P

MESH = pl.DeviceIdType.MESH
HIGHEST = lax.Precision.HIGHEST
NT = (((1,), (1,)), ((), ()))
NN = (((1,), (0,)), ((), ()))
CHUNKS = 16
CORES = 2


def gather_kernel(n, m, snap_hbm, modes_hbm, full, snap, basis, partial, landed, acc,
                  snap_sem, basis_sem, rs_send, rs_recv, ag_send, y_send, c_send, ag_recv):
    r = lax.axis_index("rows")
    t = lax.axis_index("tm")
    chips = m // CORES
    y, core = t // CORES, t % CORES
    twin = y * CORES + (1 - core)
    chunk = snap.shape[0] // CHUNKS
    piece = full.shape[1] // n

    def load(i):
        span = pl.ds(i * chunk, chunk)
        return (
            pltpu.make_async_copy(snap_hbm.at[span], snap.at[span], snap_sem.at[i]),
            pltpu.make_async_copy(modes_hbm.at[span], basis.at[span], basis_sem.at[i]),
        )

    for i in range(CHUNKS):
        for copy in load(i):
            copy.start()

    def row_peer(k):
        return lax.rem(r + k, n)

    def y_peer(d):
        return lax.rem(y + d, chips) * CORES + core

    barrier = pltpu.get_barrier_semaphore()
    for k in range(1, n):
        pl.semaphore_signal(barrier, inc=1, device_id=(row_peer(k), t), device_id_type=MESH)
    for d in range(1, chips):
        pl.semaphore_signal(barrier, inc=1, device_id=(r, y_peer(d)), device_id_type=MESH)
    pl.semaphore_signal(barrier, inc=1, device_id=(r, twin), device_id_type=MESH)

    acc[...] = jnp.zeros_like(acc)
    for i in range(CHUNKS):
        for copy in load(i):
            copy.wait()
        span = pl.ds(i * chunk, chunk)
        acc[...] += lax.dot_general(
            snap[span, :], basis[span, :], (((0,), (0,)), ((), ())),
            preferred_element_type=jnp.float32,
        )
    partial[...] = acc[...].T

    pl.semaphore_wait(barrier, n - 1 + chips - 1 + 1)

    def rows_of(j):
        return pl.ds(pl.multiple_of(j * piece, piece), piece)

    scatter = []
    for k in range(1, n):
        j = row_peer(k)
        copy = pltpu.make_async_remote_copy(
            src_ref=partial.at[rows_of(j)], dst_ref=landed.at[n - k],
            send_sem=rs_send.at[k], recv_sem=rs_recv.at[n - k],
            device_id=(j, t), device_id_type=MESH,
        )
        copy.start()
        scatter.append(copy)

    def arrival(k):
        return pltpu.make_async_remote_copy(
            src_ref=landed.at[k], dst_ref=landed.at[k],
            send_sem=rs_send.at[k], recv_sem=rs_recv.at[k],
            device_id=(row_peer(k), t), device_id_type=MESH,
        )

    total = partial[rows_of(r), :]
    for k in range(1, n):
        arrival(k).wait_recv()
        total = total + landed[k]
    full[t, rows_of(r), :] = total

    def send(block, j, sem, to):
        return pltpu.make_async_remote_copy(
            src_ref=full.at[block, rows_of(j)], dst_ref=full.at[block, rows_of(j)],
            send_sem=sem, recv_sem=ag_recv.at[block, j],
            device_id=to, device_id_type=MESH,
        )

    started = []

    def go(copy):
        copy.start()
        started.append(copy)

    for k in range(1, n):
        go(send(t, r, ag_send.at[k], (row_peer(k), t)))
    for k in range(n):
        j = row_peer(n - k) if k else r
        if k:
            send(t, j, ag_send.at[k], (j, t)).wait_recv()
        for d in range(1, chips):
            go(send(t, j, y_send.at[d, k], (r, y_peer(d))))
        go(send(t, j, c_send.at[0, k], (r, twin)))
    for d in range(1, chips):
        block = y_peer(chips - d)
        for k in range(n):
            j = row_peer(n - k) if k else r
            send(block, j, y_send.at[d, k], (r, block)).wait_recv()
            go(send(block, j, c_send.at[d, k], (r, twin)))
    for d in range(chips):
        block = lax.rem(y + d, chips) * CORES + (1 - core)
        for k in range(n):
            j = row_peer(k) if k else r
            send(block, j, c_send.at[d, k], (r, twin)).wait_recv()
    for copy in scatter + started:
        copy.wait_send()


def gathered_coords(n, m, snapshots, modes):
    depth, block = snapshots.shape
    width = modes.shape[1]
    chips = m // CORES
    dma = pltpu.SemaphoreType.DMA
    return pl.pallas_call(
        functools.partial(gather_kernel, n, m),
        out_shape=jax.ShapeDtypeStruct((m, width, block), jnp.float32),
        in_specs=[pl.BlockSpec(memory_space=pl.ANY)] * 2,
        out_specs=pl.BlockSpec(memory_space=pltpu.VMEM),
        scratch_shapes=[
            pltpu.VMEM((depth, block), snapshots.dtype),
            pltpu.VMEM((depth, width), modes.dtype),
            pltpu.VMEM((width, block), jnp.float32),
            pltpu.VMEM((n, width // n, block), jnp.float32),
            pltpu.VMEM((block, width), jnp.float32),
            dma((CHUNKS,)),
            dma((CHUNKS,)),
            dma((n,)),
            dma((n,)),
            dma((n,)),
            dma((chips, n)),
            dma((chips, n)),
            dma((m, n)),
        ],
        compiler_params=pltpu.CompilerParams(
            collective_id=0, has_side_effects=True, vmem_limit_bytes=44 * 2**20
        ),
    )(snapshots, modes)


def solve_kernel(m, coords, vectors, values, operator, residual, norms, grams, work):
    width, block = coords.shape[1:]
    total = m * block
    scale = jnp.float32(total - 1)
    series = jnp.concatenate([coords[i] for i in range(m)], axis=1)
    column = lax.broadcasted_iota(jnp.int32, (width, total), 1)
    lead = jnp.where(column < total - 1, series, 0.0)
    trail = pltpu.roll(series, total - 1, 1)

    def exact(a, b, dims=NN):
        return lax.dot_general(a, b, dims, precision=HIGHEST, preferred_element_type=jnp.float32)

    def rough(a, b):
        return lax.dot_general(
            a.astype(jnp.bfloat16), b.astype(jnp.bfloat16), NN, preferred_element_type=jnp.float32
        )

    row = lax.broadcasted_iota(jnp.int32, (width, width), 0)
    col = lax.broadcasted_iota(jnp.int32, (width, width), 1)
    eye = jnp.where(row == col, 1.0, 0.0)
    cross = exact(trail, lead, NT) / scale
    gram = exact(lead, lead, NT) / scale + eye
    grams[0] = gram
    grams[1] = cross

    mean = jnp.sum(gram * eye) / width
    square = jnp.sum(gram * gram) / width
    spread = jnp.sqrt(jnp.full((1, 1), jnp.maximum(square - mean * mean, 0.0)))
    top = jnp.maximum(mean + 3.0 * spread, 1.001)
    middle, half = (top + 1.0) * 0.5, (top - 1.0) * 0.5
    guess = (2.0 * middle * eye - gram) * (2.0 / (2.0 * middle * middle - half * half))
    error = eye - rough(guess, gram)
    inverse = guess + rough(error, guess)
    error = rough(error, error)
    inverse = inverse + rough(error, inverse)
    error = rough(error, error)
    inverse = inverse + rough(error, inverse)
    grams[2] = inverse

    first = rough(cross, inverse)
    operator[...] = first
    rest = cross - exact(first, gram)
    grams[3] = rest

    def size(a):
        return jnp.sum(a * a)

    def more(state):
        step, left = state
        return jnp.logical_and(step < 6, jnp.logical_not(left <= 4e-10))

    def refine(state):
        step, _ = state
        better = operator[...] + rough(grams[3], grams[2])
        operator[...] = better
        rest = grams[1] - exact(better, grams[0])
        grams[3] = rest
        ratio = jnp.full((1, 1), size(rest)) / jnp.maximum(size(better), 1e-30)
        return step + 1, ratio[0, 0]

    _, left = lax.while_loop(more, refine, (jnp.int32(0), jnp.float32(1.0)))
    settled = left <= 4e-10

    @pl.when(settled)
    def _():
        operator[...] += rough(grams[3], grams[2])

    @pl.when(jnp.logical_not(settled))
    def _():
        work[pl.ds(0, width), :] = grams[0]
        work[pl.ds(width, width), :] = grams[1]
        lane = lax.broadcasted_iota(jnp.int32, (2 * width, width), 1)

        def eliminate(k, carry):
            whole = work[...]
            here = lane == k
            lever = jnp.sum(jnp.where(here, whole, 0.0), axis=1, keepdims=True)
            pivot_row = work[pl.ds(k, 1), :]
            pivot = jnp.sum(jnp.where(here[:1], pivot_row, 0.0), axis=1, keepdims=True)
            scaled = lever / pivot
            work[...] = jnp.where(here, scaled, whole - scaled * pivot_row)
            return carry

        lax.fori_loop(0, width, eliminate, 0)
        operator[...] = work[pl.ds(width, width), :]

    image = exact(vectors[...], operator[...], NT)
    count = vectors.shape[0]
    for k in range(count):
        line = image[k : k + 1, :] - values[k] * vectors[k : k + 1, :]
        residual[k : k + 1, :] = line
        length = jnp.sqrt(jnp.sum(line * line, axis=1, keepdims=True) + 1e-06)
        norms[k] = length[0, 0]


def solved(m, coords, vectors, values):
    width = coords.shape[1]
    vmem = pl.BlockSpec(memory_space=pltpu.VMEM)
    smem = pl.BlockSpec(memory_space=pltpu.SMEM)
    return pl.pallas_call(
        functools.partial(solve_kernel, m),
        out_shape=(
            jax.ShapeDtypeStruct((width, width), jnp.float32),
            jax.ShapeDtypeStruct(vectors.shape, jnp.float32),
            jax.ShapeDtypeStruct(values.shape, jnp.float32),
        ),
        in_specs=[vmem, vmem, smem],
        out_specs=(vmem, vmem, smem),
        scratch_shapes=[
            pltpu.VMEM((4, width, width), jnp.float32),
            pltpu.VMEM((2 * width, width), jnp.float32),
        ],
    )(coords, vectors, values)


def solution(mesh):
    n, m = mesh.shape["rows"], mesh.shape["tm"]

    def body(snapshots, modes, eig_vectors, eig_values):
        coords = gathered_coords(n, m, snapshots, modes)
        return solved(m, coords, eig_vectors, eig_values)

    return jax.shard_map(
        body,
        mesh=mesh,
        in_specs=(P("rows", "tm"), P("rows", None), P(), P()),
        out_specs=(P(), P(), P()),
        check_vma=False,
    )
```

time: 174 us -> 83.5 us (0.48)
  Pallas kernels: 0 us -> 78.5 us
  waiting for transfers between devices: 73.3 us -> 0 us
  other arithmetic: 54.2 us -> 0 us
  matrix products: 17.9 us -> 0 us
  between operations: 15.5 us -> 0.65 us
  blocking collectives: 7.53 us -> 0 us
    pallas_call x0 -> x2, Pallas kernels: none -> 78.5 us  [the longest x1 53.8 us: solved(): pl.pallas_call(functools.partial(solve_kernel, m), out_shape=(jax.ShapeDt...]
    psum x1 -> x0, waiting for transfers between devices: 73.3 us -> none  [body(): coords = lax.psum(partial_value, 'rows')]
    another operation x9 -> x0, other arithmetic: 53.7 us -> none  [the longest x6 33.9 us: body(): factor = jnp.linalg.cholesky(gram)]
    dot_general x4 -> x0, matrix products: 15.6 us -> none  [the longest x1 13.4 us: body(): jnp.einsum('mr,mt->rt', modes, snapshots, preferred_element_type=jnp.floa...]
    all_gather x1 -> x0, blocking collectives: 7.53 us -> none  [body(): series = lax.all_gather(coords, 'tm', axis=1, tiled=True)]
    another operation x9 -> x0, local copies, waits for them, and re-layouts: 4.05 us -> none
    unnamed x5 -> x4, local copies, waits for them, and re-layouts: 0.85 us -> 4.15 us
    another operation x8 -> x0, matrix products: 2.32 us -> none  [the longest x6 1.85 us: body(): operator = jax.scipy.linalg.cho_solve((factor, True), cross.T).T]
  transfers between devices with their start and end apart: 1 -> 0, of which waited for: 1 -> 0; matrix products, arithmetic and copies ran while one was open for 0% -> 0% of each run, Pallas kernels for 0% -> 0%
where the time goes in v1:
time: 83.5 us; the launch traced here: 83.3 us
  Pallas kernels  78.5 us (94%)
  local copies, waits for them, and re-layouts  4.15 us (5%)
    pallas_call x1, Pallas kernels, solved(): pl.pallas_call(functools.partial(solve_kernel, m), out_shape=(jax.ShapeDt...  53.8 us
    pallas_call x1, Pallas kernels, gathered_coords(): pl.pallas_call(functools.partial(gather_kernel, n, m), out_shape=jax.Shap...  24.7 us
    unnamed x4, local copies, waits for them, and re-layouts  4.15 us

profile of v1, /device:TPU:0, one launch (start us, length us, event | category | flops | bytes accessed | tf_op | source)
XLA Modules:
  0.0 83.3 jit_solution(6757841757484954266)
XLA Ops:
  0.6 0.0 copy-start
  0.6 3.4 %copy-done = bf16[32768,128]{1,0:T(8,128)(2,1)S(1)} copy-done((bf16[32768,128]{1,0:T(8,128)(2,1)S(1)}, bf16[32768,128]{1,0:T(8,128)(2,1)}, u32[]{:S(2)}) %copy-start) | copy-done | bytes 8388632
  4.0 24.7 %shard_map.67.coords = f32[4,256,128]{2,1,0:T(8,128)S(1)} custom-call(bf16[32768,128]{1,0:T(8,128)(2,1)S(1)} %copy-done, bf16[32768,256]{1,0:T(8,128)(2,1)} %modes_hbm.1), custom_call_target="tpu_custom_call" | custom-call | tf_op jit(solution)/shard_map/pallas_call | solution.py:134
  28.7 0.0 copy-start.1
  28.7 0.8 copy-done.1
  29.5 53.8 %shard_map.68 = (f32[256,256]{1,0:T(8,128)}, f32[3,256]{1,0:T(4,128)}, f32[3]{0:T(128)}) custom-call(f32[4,256,128]{2,1,0:T(8,128)} %copy-done.1, f32[3,256]{1,0:T(4,128)} %vectors.1, f32[3]{0:T(128)} %values.1), custom_call_target="tpu_custom_call" | custom-call | tf_op jit(solution)/shard_map/pallas_call | solution.py:259
Async XLA Ops:
  0.6 3.4 %copy-start = (bf16[32768,128]{1,0:T(8,128)(2,1)S(1)}, bf16[32768,128]{1,0:T(8,128)(2,1)}, u32[]{:S(2)}) copy-start(bf16[32768,128]{1,0:T(8,128)(2,1)} %snap_hbm.1) | copy-start | bytes 25165828
  28.7 0.8 copy-start.1

commit v2 on v1

--- a/solution.py
+++ b/solution.py
@@ -152,7 +152,7 @@
             dma((m, n)),
         ],
         compiler_params=pltpu.CompilerParams(
-            collective_id=0, has_side_effects=True, vmem_limit_bytes=44 * 2**20
+            collective_id=0, has_side_effects=True, vmem_limit_bytes=60 * 2**20
         ),
     )(snapshots, modes)
 
@@ -206,7 +206,7 @@
 
     def more(state):
         step, left = state
-        return jnp.logical_and(step < 6, jnp.logical_not(left <= 4e-10))
+        return jnp.logical_and(step < 6, jnp.logical_not(left <= 1e-8))
 
     def refine(state):
         step, _ = state
@@ -218,7 +218,7 @@
         return step + 1, ratio[0, 0]
 
     _, left = lax.while_loop(more, refine, (jnp.int32(0), jnp.float32(1.0)))
-    settled = left <= 4e-10
+    settled = left <= 1e-8
 
     @pl.when(settled)
     def _():

time: 83.5 us -> 82 us (0.982)
  local copies, waits for them, and re-layouts: 4.15 us -> 0 us
  Pallas kernels: 78.5 us -> 81.2 us
    unnamed x4 -> x0, local copies, waits for them, and re-layouts: 4.15 us -> none
    pallas_call x1, Pallas kernels: 24.7 us -> 27.4 us  [gathered_coords(): pl.pallas_call(functools.partial(gather_kernel, n, m), out_shape=jax.Shap...]
where the time goes in v2:
time: 82 us; the launch traced here: 81.9 us
  Pallas kernels  81.2 us (99%)
    pallas_call x1, Pallas kernels, solved(): pl.pallas_call(functools.partial(solve_kernel, m), out_shape=(jax.ShapeDt...  53.8 us
    pallas_call x1, Pallas kernels, gathered_coords(): pl.pallas_call(functools.partial(gather_kernel, n, m), out_shape=jax.Shap...  27.4 us

profile of v2, /device:TPU:0, one launch (start us, length us, event | category | flops | bytes accessed | tf_op | source)
XLA Modules:
  0.0 81.9 jit_solution(16618230796445126002)
XLA Ops:
  0.6 27.4 %shard_map.67.coords = f32[4,256,128]{2,1,0:T(8,128)} custom-call(bf16[32768,128]{1,0:T(8,128)(2,1)} %snap_hbm.1, bf16[32768,256]{1,0:T(8,128)(2,1)} %modes_hbm.1), custom_call_target="tpu_custom_call" | custom-call | tf_op jit(solution)/shard_map/pallas_call | solution.py:134
  28.0 53.8 %shard_map.68 = (f32[256,256]{1,0:T(8,128)}, f32[3,256]{1,0:T(4,128)}, f32[3]{0:T(128)}) custom-call(f32[4,256,128]{2,1,0:T(8,128)} %shard_map.67.coords, f32[3,256]{1,0:T(4,128)} %vectors.1, f32[3]{0:T(128)} %values.1), custom_call_target="tpu_custom_call" | custom-call | tf_op jit(solution)/shard_map/pallas_call | solution.py:259

commit v3 on v2

--- a/solution.py
+++ b/solution.py
@@ -102,8 +102,6 @@
         copy.start()
         started.append(copy)
 
-    for k in range(1, n):
-        go(send(t, r, ag_send.at[k], (row_peer(k), t)))
     for k in range(n):
         j = row_peer(n - k) if k else r
         if k:
@@ -111,6 +109,9 @@
         for d in range(1, chips):
             go(send(t, j, y_send.at[d, k], (r, y_peer(d))))
         go(send(t, j, c_send.at[0, k], (r, twin)))
+        if k == 0:
+            for hop in range(1, n):
+                go(send(t, r, ag_send.at[hop], (row_peer(hop), t)))
     for d in range(1, chips):
         block = y_peer(chips - d)
         for k in range(n):
@@ -177,8 +178,9 @@
     row = lax.broadcasted_iota(jnp.int32, (width, width), 0)
     col = lax.broadcasted_iota(jnp.int32, (width, width), 1)
     eye = jnp.where(row == col, 1.0, 0.0)
-    cross = exact(trail, lead, NT) / scale
-    gram = exact(lead, lead, NT) / scale + eye
+    both = exact(jnp.concatenate([trail, lead], axis=0), lead, NT) / scale
+    cross = both[:width]
+    gram = both[width:] + eye
     grams[0] = gram
     grams[1] = cross
 

time: 82 us -> 82.2 us (level)
  no operation moved by 1% of the time
where the time goes in v3:
time: 82.2 us; the launch traced here: 82 us
  Pallas kernels  81.4 us (99%)
    pallas_call x1, Pallas kernels, solved(): pl.pallas_call(functools.partial(solve_kernel, m), out_shape=(jax.ShapeDt...  54 us
    pallas_call x1, Pallas kernels, gathered_coords(): pl.pallas_call(functools.partial(gather_kernel, n, m), out_shape=jax.Shap...  27.4 us

profile of v3, /device:TPU:0, one launch (start us, length us, event | category | flops | bytes accessed | tf_op | source)
XLA Modules:
  0.0 82.0 jit_solution(11424845167830044674)
XLA Ops:
  0.6 27.4 %shard_map.67.coords = f32[4,256,128]{2,1,0:T(8,128)} custom-call(bf16[32768,128]{1,0:T(8,128)(2,1)} %snap_hbm.1, bf16[32768,256]{1,0:T(8,128)(2,1)} %modes_hbm.1), custom_call_target="tpu_custom_call" | custom-call | tf_op jit(solution)/shard_map/pallas_call | solution.py:135
  28.0 54.0 %shard_map.68 = (f32[256,256]{1,0:T(8,128)}, f32[3,256]{1,0:T(4,128)}, f32[3]{0:T(128)}) custom-call(f32[4,256,128]{2,1,0:T(8,128)} %shard_map.67.coords, f32[3,256]{1,0:T(4,128)} %vectors.1, f32[3]{0:T(128)} %values.1), custom_call_target="tpu_custom_call" | custom-call | tf_op jit(solution)/shard_map/pallas_call | solution.py:261
